TPU v7x, 128 devices: a whole 4x4x4 slice. The times are simulated.
128 devices in a mesh: wide: 16 (over z_hi, x, core), narrow: 8 (over z_lo, y).
Axes of the slice: x: 4, y: 4, z: 4 (z_hi: 2, z_lo: 2; z = z_hi * 2 + z_lo), core: 2. Of those that a mesh axis runs over, the one named last changes fastest.
Arguments:
- points: float32 [8, 32768], P(None, 'narrow'), may hold values from 0 to 1
- scales: float32 [8], replicated, may hold values from 2 to 6
- frequencies: float32 [8, 32768], P(None, 'wide'), may hold values from -24 to 24
- phases: float32 [32768], P('wide'), may hold values from -3.140625 to 3.140625
- feature_weights: bfloat16 [64, 32768], P(None, 'wide'), may hold values from -6 to 6
- targets: float32 [32768], P(('narrow', 'wide')), may hold values from -6 to 6
- noise: float32 [64, 32768], P(None, ('narrow', 'wide')), may hold values from -1.8 to 1.8
- inverses: float32 [2, 8192, 8192], P(None, 'wide', 'narrow'), may hold values from -0.01767767 to 1.0176777
- groups: int32 [2, 64], replicated, may hold values from 0 to 255, as said below
Outputs:
- residual: float32 [64, 32768], P(None, ('narrow', 'wide'))
- weights: float32 [2, 64, 8192], P(None, None, 'wide')
Inputs may be any that keep to these rules, and one draw needn't show every extreme that they name: All entries differ; each names the group of points g * 128 to g * 128 + 127. In every block, the entries n * 8 to (n + 1) * 8 - 1 name groups of narrow index n's points, that is groups n * 32 to (n + 1) * 32 - 1.
All inputs are finite; a program needn't handle non-finite values.
Results may differ from a plain program's by a relative error of at most 0.00065.
Values may be sent and summed in bfloat16 or wider, within the bound.
A program may use at most 128 MiB of HBM per device.

v0:
```python
import math

import jax
import jax.numpy as jnp
from jax import lax
from jax.sharding import PartitionSpec as P

FEATURES = 32768
GROUP = 128
BLOCKS = 2


NOISE_VAR = 0.1
ROOT_FIVE = math.sqrt(5.0)
HIGH = lax.Precision.HIGHEST


def laid_out(pieces, dim):
    pieces = jnp.moveaxis(pieces, 0, dim)
    dims = pieces.shape
    return pieces.reshape(*dims[:dim], dims[dim] * dims[dim + 1], *dims[dim + 2 :])


def sent_to_all(shard, axis):
    copies = jnp.broadcast_to(shard, (lax.axis_size(axis), *shard.shape))
    return lax.all_to_all(copies, axis, split_axis=0, concat_axis=0, tiled=True)


def gathered_copies(shard, axis, dim):
    return laid_out(sent_to_all(shard, axis), dim)


def cut_along(shard, dim, peers):
    dims = shard.shape
    pieces = shard.reshape(*dims[:dim], peers, dims[dim] // peers, *dims[dim + 1 :])
    return jnp.moveaxis(pieces, dim, 0)


def summed_on_arrival(shard, axis, dim):
    pieces = cut_along(shard, dim, lax.axis_size(axis))
    arrived = lax.all_to_all(pieces, axis, split_axis=0, concat_axis=0, tiled=True)
    return arrived.sum(axis=0)


def taken_together(shard, axis):
    everything = sent_to_all(shard, axis)
    return jnp.sum(everything, axis=0)


def matern_tile(rows_coords, cols_coords, row_ids, col_ids):
    dist_sq = jnp.zeros((rows_coords.shape[1], cols_coords.shape[1]), jnp.float32)
    for coord in range(rows_coords.shape[0]):
        differ = rows_coords[coord][:, None] - cols_coords[coord][None, :]
        dist_sq = dist_sq + differ * differ
    scaled = ROOT_FIVE * jnp.sqrt(dist_sq)
    values = (1.0 + scaled + scaled * scaled / 3.0) * jnp.exp(-scaled)
    return values + jnp.where(row_ids[:, None] == col_ids[None, :], NOISE_VAR, 0.0)


def prior_terms(points_here, freq_part, phase_part, weights_part):
    width = points_here.shape[1]
    block = math.gcd(width, 1024)
    output = jnp.zeros((weights_part.shape[0], width), jnp.float32)

    def prior_one_block(index, output):
        begin = index * block
        coords = lax.dynamic_slice_in_dim(points_here, begin, block, 1)
        angles = (
            lax.dot_general(
                freq_part,
                coords,
                (((0,), (0,)), ((), ())),
                precision=HIGH,
                preferred_element_type=jnp.float32,
            )
            + phase_part[:, None]
        )
        features = jnp.cos(angles).astype(jnp.bfloat16)
        partial_sum = jnp.dot(weights_part, features, preferred_element_type=jnp.float32)
        return lax.dynamic_update_slice_in_dim(output, partial_sum, begin, 1)

    return lax.fori_loop(0, width // block, prior_one_block, output)


def kernel_terms(update, row_coords, row_ids, col_coords, col_ids):
    width = col_coords.shape[1]
    block = math.gcd(width, 2048)
    output = jnp.zeros((update.shape[0], width), jnp.float32)

    def kernel_one_block(index, output):
        begin = index * block
        tile = matern_tile(
            row_coords,
            lax.dynamic_slice_in_dim(col_coords, begin, block, 1),
            row_ids,
            lax.dynamic_slice_in_dim(col_ids, begin, block, 0),
        )
        product = jnp.dot(update, tile, precision=HIGH, preferred_element_type=jnp.float32)
        return lax.dynamic_update_slice_in_dim(output, product, begin, 1)

    return lax.fori_loop(0, width // block, kernel_one_block, output)


def spread_rows(residual):
    return gathered_copies(residual, "wide", 1)


def on_device(
    points, scales, frequencies, phases, feature_weights, targets, noise, inverses, groups
):
    wide_count = lax.axis_size("wide")
    narrow_count = lax.axis_size("narrow")
    wide_here = lax.axis_index("wide")
    narrow_here = lax.axis_index("narrow")
    shard_width = points.shape[1]
    all_points = gathered_copies(points, "narrow", 1)
    terms = prior_terms(points, frequencies, phases, feature_weights)
    prior = summed_on_arrival(terms, "wide", 1)
    residual = targets[None, :] - math.sqrt(2.0 / FEATURES) * prior - noise
    scaled_all = scales[:, None] * all_points
    scaled_own = lax.dynamic_slice_in_dim(scaled_all, narrow_here * shard_width, shard_width, 1)
    col_ids = narrow_here * shard_width + jnp.arange(shard_width, dtype=jnp.int32)
    slice_groups = groups.shape[1] // narrow_count
    row_groups = groups.shape[1] // wide_count
    shard_groups = shard_width // GROUP
    member_offsets = jnp.arange(GROUP, dtype=jnp.int32)
    whole = spread_rows(residual)
    weight_list = []
    for block_index in range(BLOCKS):
        block_groups = groups[block_index]
        col_groups = (
            lax.dynamic_slice_in_dim(block_groups, narrow_here * slice_groups, slice_groups, 0)
            - narrow_here * shard_groups
        )
        stacked = whole.reshape(whole.shape[0], shard_groups, GROUP)
        picked = jnp.take(stacked, col_groups, axis=1).reshape(whole.shape[0], slice_groups * GROUP)
        partial_sum = lax.dot_general(
            picked,
            inverses[block_index],
            (((1,), (1,)), ((), ())),
            precision=HIGH,
            preferred_element_type=jnp.float32,
        )
        update = taken_together(partial_sum, "narrow")
        weight_list.append(update)
        row_group_ids = lax.dynamic_slice_in_dim(
            block_groups, wide_here * row_groups, row_groups, 0
        )
        row_ids = (row_group_ids[:, None] * GROUP + member_offsets[None, :]).reshape(-1)
        row_coords = jnp.take(scaled_all, row_ids, axis=1)
        terms = kernel_terms(update, row_coords, row_ids, scaled_own, col_ids)
        residual = residual - summed_on_arrival(terms, "wide", 1)
        if block_index + 1 < BLOCKS:
            whole = spread_rows(residual)
    return (residual, jnp.stack(weight_list))


def solution(mesh):
    in_specs = (
        P(None, "narrow"),
        P(),
        P(None, "wide"),
        P("wide"),
        P(None, "wide"),
        P(("narrow", "wide")),
        P(None, ("narrow", "wide")),
        P(None, "wide", "narrow"),
        P(),
    )
    out_specs = (P(None, ("narrow", "wide")), P(None, None, "wide"))
    return jax.shard_map(
        on_device, mesh=mesh, in_specs=in_specs, out_specs=out_specs, check_vma=False
    )
```

profile of v0, /device:TPU:1, one launch (start us, length us, event | category | flops | bytes accessed | tf_op | source)
XLA Modules:
  0.0 392.1 jit_solution(17785193199646789398)
XLA Ops:
  0.7 148.4 %while.41 = (s32[]{:T(128)}, f32[64,4096]{1,0:T(8,128)S(1)}, f32[8,4096]{1,0:T(8,128)}, f32[8,2048]{1,0:T(8,128)}, f32[2048]{0:T(1024)}, /*index=5*/bf16[64,2048...) while((s32[]{:T(128)}, f32[64,4096]{1,0:T(8,128)S(1)}, f32[8,4096]{1,0:T(8,128)}, ...), condition=%wide.region_1.0_spmd, body=%wide.region_0.0_spmd.sunk | while | flops 473956352 | bytes 10068151 | solution.py:82
  0.7 35.7 %cosine_convert_fusion.2 = bf16[1024,2048]{1,0:T(8,128)(2,1)S(1)} fusion(f32[8,2048]{1,0:T(8,128)} %get-tuple-element.762, f32[2048]{0:T(1024)} %get-tuple-element.763, f32[8,4096]{1,0:T(8,128)} %get-tuple-element.761, s32[]{:T(128)S(6)} %select_n.128), kind=kOutput, calls=%fused_computation.6.clone.1 | convolution fusion | flops 205520896 | bytes 4300804 | tf_op jit(solution)/shard_map/while/body/eval_jaxpr/dot_general | solution.py:69
  37.8 35.6 %cosine_convert_fusion.2 = bf16[1024,2048]{1,0:T(8,128)(2,1)S(1)} fusion(f32[8,2048]{1,0:T(8,128)} %get-tuple-element.762, f32[2048]{0:T(1024)} %get-tuple-element.763, f32[8,4096]{1,0:T(8,128)} %get-tuple-element.761, s32[]{:T(128)S(6)} %select_n.128), kind=kOutput, calls=%fused_computation.6.clone.1 | convolution fusion | flops 205520896 | bytes 4300804 | tf_op jit(solution)/shard_map/while/body/eval_jaxpr/dot_general | solution.py:69
  74.9 35.7 %cosine_convert_fusion.2 = bf16[1024,2048]{1,0:T(8,128)(2,1)S(1)} fusion(f32[8,2048]{1,0:T(8,128)} %get-tuple-element.762, f32[2048]{0:T(1024)} %get-tuple-element.763, f32[8,4096]{1,0:T(8,128)} %get-tuple-element.761, s32[]{:T(128)S(6)} %select_n.128), kind=kOutput, calls=%fused_computation.6.clone.1 | convolution fusion | flops 205520896 | bytes 4300804 | tf_op jit(solution)/shard_map/while/body/eval_jaxpr/dot_general | solution.py:69
  112.0 35.6 %cosine_convert_fusion.2 = bf16[1024,2048]{1,0:T(8,128)(2,1)S(1)} fusion(f32[8,2048]{1,0:T(8,128)} %get-tuple-element.762, f32[2048]{0:T(1024)} %get-tuple-element.763, f32[8,4096]{1,0:T(8,128)} %get-tuple-element.761, s32[]{:T(128)S(6)} %select_n.128), kind=kOutput, calls=%fused_computation.6.clone.1 | convolution fusion | flops 205520896 | bytes 4300804 | tf_op jit(solution)/shard_map/while/body/eval_jaxpr/dot_general | solution.py:69
  150.1 25.5 %all_to_all.40 = f32[16,64,256]{2,1,0:T(8,128)S(1)} all-to-all(f32[16,64,256]{2,1,0:T(8,128)S(1)} %copy.50), channel_id=1, replica_groups=mesh['wide'=16,'narrow'=8] {'wide'}, dimensions={0} | all-to-all | bytes 2097152 | tf_op jit(solution)/shard_map/all_to_all | solution.py:41
  176.7 4.6 %all-to-all-start.1 = ((f32[8,8,4096]{2,1,0:T(8,128)}), f32[8,8,4096]{2,1,0:T(8,128)S(1)}, u32[]{:S(2)}, u32[]{:S(2)}) async-start(f32[8,8,4096]{2,1,0:T(8,128)} %broadcast_in_dim.78), calls=%async_computation.1 | async-start | bytes 2097152 | tf_op jit(solution)/shard_map/all_to_all | solution.py:26
  181.5 15.7 %all-to-all-done.1 = f32[8,8,4096]{2,1,0:T(8,128)S(1)} async-done(((f32[8,8,4096]{2,1,0:T(8,128)}), f32[8,8,4096]{2,1,0:T(8,128)S(1)}, u32[]{:S(2)}, u32[]{:S(2)}) %all-to-all-start.1) | async-done | bytes 1048608 | tf_op jit(solution)/shard_map/all_to_all | solution.py:26
  198.3 4.9 %all-to-all-start.2 = ((f32[16,64,256]{2,1,0:T(8,128)}), f32[16,64,256]{2,1,0:T(8,128)S(1)}, u32[]{:S(2)}, u32[]{:S(2)}) async-start(f32[16,64,256]{2,1,0:T(8,128)} %broadcast_in_dim.79), calls=%async_computation.2 | async-start | bytes 2097152 | tf_op jit(solution)/shard_map/all_to_all | solution.py:26
  203.5 8.2 %copy.51 = f32[8,8,4096]{0,2,1:T(8,128)} copy(f32[8,8,4096]{2,0,1:T(8,128)S(1)} %bitcast.204) | data formatting | bytes 2097152 | tf_op jit(solution)/shard_map/transpose | solution.py:19
  211.7 8.7 %all-to-all-done.2 = f32[16,64,256]{2,1,0:T(8,128)S(1)} async-done(((f32[16,64,256]{2,1,0:T(8,128)}), f32[16,64,256]{2,1,0:T(8,128)S(1)}, u32[]{:S(2)}, u32[]{:S(2)}) %all-to-all-start.2) | async-done | bytes 1048608 | tf_op jit(solution)/shard_map/all_to_all | solution.py:26
  222.3 3.7 fusion.149
  227.2 3.8 all-to-all-start.3
  231.0 11.3 %bitcast_multiply_fusion = f32[8,32768]{0,1:T(8,128)} fusion(f32[8,8,4096]{0,2,1:T(8,128)} %copy.51, f32[8]{0:T(128)S(1)} %copy-done.5), kind=kLoop, calls=%fused_computation.147 | loop fusion | flops 262144 | bytes 2097184 | tf_op jit(solution)/shard_map/mul | solution.py:120
  242.3 6.8 %gather_fusion = f32[512,8]{1,0:T(8,128)S(1)} fusion(f32[8,32768]{0,1:T(8,128)} %bitcast_multiply_fusion, s32[1024]{0:T(1024)S(1)} %pad_clamp_fusion.3), kind=kCustom, calls=%fused_computation.clone | custom fusion | bytes 34816 | tf_op jit(solution)/shard_map/jit(_take)/gather | solution.py:150
  249.3 1.7 constant_dynamic-slice_fusion.5
  251.8 16.9 %while.42 = (s32[]{:T(128)}, f32[64,4096]{1,0:T(8,128)S(1)}, f32[8,512]{1,0:T(8,128)S(1)}, f32[8,4096]{1,0:T(8,128)S(1)}, s32[4096]{0:T(1024)S(1)}, /*index=5*/f...) while((s32[]{:T(128)}, f32[64,4096]{1,0:T(8,128)S(1)}, ...), condition=%wide.region_5.8_spmd.clone, body=%wide.region_4.0_spmd.clone.sunk | while | flops 839909888 | bytes 930143 | solution.py:101
  252.1 8.1 %fusion.194 = f32[64,4096]{1,0:T(8,128)S(1)} fusion(f32[64,4096]{1,0:T(8,128)S(1)} %get-tuple-element.788, s32[]{:T(128)S(6)} %select_n.130, f32[64,512]{1,0:T(8,128)S(1)} %get-tuple-element.810, s32[2048]{0:T(1024)S(1)} %dynamic_slice.92, f32[2048]{0:T(1024)S(1)} %bitcast.222, f32[512]{0:T(512)S(1)} %bitcast.232, f32[2048]{0:T(1024)S(1)} %bitcast.216, ...), kind=kOutput, calls=%fused_computation.48.clone.1 | convolution fusion | flops 839909376 | bytes 747524 | tf_op jit(solution)/shard_map/while/body/eval_jaxpr/dot_general | solution.py:98
  260.6 8.1 %fusion.194 = f32[64,4096]{1,0:T(8,128)S(1)} fusion(f32[64,4096]{1,0:T(8,128)S(1)} %get-tuple-element.788, s32[]{:T(128)S(6)} %select_n.130, f32[64,512]{1,0:T(8,128)S(1)} %get-tuple-element.810, s32[2048]{0:T(1024)S(1)} %dynamic_slice.92, f32[2048]{0:T(1024)S(1)} %bitcast.222, f32[512]{0:T(512)S(1)} %bitcast.232, f32[2048]{0:T(1024)S(1)} %bitcast.216, ...), kind=kOutput, calls=%fused_computation.48.clone.1 | convolution fusion | flops 839909376 | bytes 747524 | tf_op jit(solution)/shard_map/while/body/eval_jaxpr/dot_general | solution.py:98
  269.7 19.9 %all_to_all.41 = f32[16,64,256]{2,1,0:T(8,128)S(1)} all-to-all(f32[16,64,256]{2,1,0:T(8,128)S(1)} %copy.57), channel_id=1, replica_groups=mesh['wide'=16,'narrow'=8] {'wide'}, dimensions={0} | all-to-all | bytes 2097152 | tf_op jit(solution)/shard_map/all_to_all | solution.py:41
  290.8 14.5 %all-to-all-start.5 = ((f32[16,64,256]{2,1,0:T(8,128)}), f32[16,64,256]{2,1,0:T(8,128)S(1)}, u32[]{:S(2)}, u32[]{:S(2)}) async-start(f32[16,64,256]{2,1,0:T(8,128)} %broadcast_in_dim.81), calls=%async_computation.5 | async-start | bytes 2097152 | tf_op jit(solution)/shard_map/all_to_all | solution.py:26
  305.3 17.3 %all-to-all-done.5 = f32[16,64,256]{2,1,0:T(8,128)S(1)} async-done(((f32[16,64,256]{2,1,0:T(8,128)}), f32[16,64,256]{2,1,0:T(8,128)S(1)}, u32[]{:S(2)}, u32[]{:S(2)}) %all-to-all-start.5) | async-done | bytes 1048608 | tf_op jit(solution)/shard_map/all_to_all | solution.py:26
  324.5 3.7 fusion.147
  329.3 5.4 %all-to-all-start.6 = ((f32[8,64,512]{2,1,0:T(8,128)}), f32[8,64,512]{2,1,0:T(8,128)S(1)}, u32[]{:S(2)}, u32[]{:S(2)}) async-start(f32[8,64,512]{2,1,0:T(8,128)} %broadcast_in_dim.82), calls=%async_computation.6 | async-start | bytes 2097152 | tf_op jit(solution)/shard_map/all_to_all | solution.py:26
  334.7 6.8 %gather_fusion.2 = f32[512,8]{1,0:T(8,128)S(1)} fusion(f32[8,32768]{0,1:T(8,128)} %bitcast_multiply_fusion, s32[1024]{0:T(1024)S(1)} %pad_clamp_fusion.1), kind=kCustom, calls=%fused_computation.2.clone | custom fusion | bytes 34816 | tf_op jit(solution)/shard_map/jit(_take)/gather | solution.py:150
  341.8 8.8 %all-to-all-done.6 = f32[8,64,512]{2,1,0:T(8,128)S(1)} async-done(((f32[8,64,512]{2,1,0:T(8,128)}), f32[8,64,512]{2,1,0:T(8,128)S(1)}, u32[]{:S(2)}, u32[]{:S(2)}) %all-to-all-start.6) | async-done | bytes 1048608 | tf_op jit(solution)/shard_map/all_to_all | solution.py:26
  350.7 16.9 %while.43 = (s32[]{:T(128)}, f32[64,4096]{1,0:T(8,128)S(1)}, f32[8,512]{1,0:T(8,128)S(1)}, f32[8,4096]{1,0:T(8,128)S(1)}, s32[4096]{0:T(1024)S(1)}, /*index=5*/f...) while((s32[]{:T(128)}, f32[64,4096]{1,0:T(8,128)S(1)}, ...), condition=%wide.region_9.12_spmd.clone, body=%wide.region_8.11_spmd.clone.sunk | while | flops 839909888 | bytes 930143 | solution.py:101
  351.1 8.1 %fusion.198 = f32[64,4096]{1,0:T(8,128)S(1)} fusion(f32[64,4096]{1,0:T(8,128)S(1)} %get-tuple-element.842, s32[]{:T(128)S(6)} %select_n.132, f32[64,512]{1,0:T(8,128)S(1)} %get-tuple-element.864, s32[2048]{0:T(1024)S(1)} %dynamic_slice.93, f32[2048]{0:T(1024)S(1)} %bitcast.230, f32[512]{0:T(512)S(1)} %bitcast.240, f32[2048]{0:T(1024)S(1)} %bitcast.224, ...), kind=kOutput, calls=%fused_computation.116.clone.1 | convolution fusion | flops 839909376 | bytes 747524 | tf_op jit(solution)/shard_map/while/body/eval_jaxpr/dot_general | solution.py:98
  359.5 8.1 %fusion.198 = f32[64,4096]{1,0:T(8,128)S(1)} fusion(f32[64,4096]{1,0:T(8,128)S(1)} %get-tuple-element.842, s32[]{:T(128)S(6)} %select_n.132, f32[64,512]{1,0:T(8,128)S(1)} %get-tuple-element.864, s32[2048]{0:T(1024)S(1)} %dynamic_slice.93, f32[2048]{0:T(1024)S(1)} %bitcast.230, f32[512]{0:T(512)S(1)} %bitcast.240, f32[2048]{0:T(1024)S(1)} %bitcast.224, ...), kind=kOutput, calls=%fused_computation.116.clone.1 | convolution fusion | flops 839909376 | bytes 747524 | tf_op jit(solution)/shard_map/while/body/eval_jaxpr/dot_general | solution.py:98
  368.0 1.6 copy.63
  369.6 4.2 %all-to-all-start.7 = ((f32[16,64,256]{2,1,0:T(8,128)}), f32[16,64,256]{2,1,0:T(8,128)S(1)}, u32[]{:S(2)}, u32[]{:S(2)}) async-start(f32[16,64,256]{2,1,0:T(8,128)} %copy.63), calls=%async_computation.7 | async-start | bytes 2097152 | tf_op jit(solution)/shard_map/all_to_all | solution.py:41
  374.5 16.6 %all-to-all-done.7 = f32[16,64,256]{2,1,0:T(8,128)S(1)} async-done(((f32[16,64,256]{2,1,0:T(8,128)}), f32[16,64,256]{2,1,0:T(8,128)S(1)}, u32[]{:S(2)}, u32[]{:S(2)}) %all-to-all-start.7) | async-done | bytes 1048608 | tf_op jit(solution)/shard_map/all_to_all | solution.py:41
  (85 shorter events, 21.6 us)
Async XLA Ops:
  0.7 35.7 %copy-start = (bf16[64,2048]{1,0:T(8,128)(2,1)S(1)}, bf16[64,2048]{1,0:T(8,128)(2,1)}, u32[]{:S(2)}) copy-start(bf16[64,2048]{1,0:T(8,128)(2,1)} %get-tuple-element.764) | copy-start | bytes 786436 | tf_op jit(solution)/shard_map/while
  37.8 35.7 %copy-start = (bf16[64,2048]{1,0:T(8,128)(2,1)S(1)}, bf16[64,2048]{1,0:T(8,128)(2,1)}, u32[]{:S(2)}) copy-start(bf16[64,2048]{1,0:T(8,128)(2,1)} %get-tuple-element.764) | copy-start | bytes 786436 | tf_op jit(solution)/shard_map/while
  74.9 35.7 %copy-start = (bf16[64,2048]{1,0:T(8,128)(2,1)S(1)}, bf16[64,2048]{1,0:T(8,128)(2,1)}, u32[]{:S(2)}) copy-start(bf16[64,2048]{1,0:T(8,128)(2,1)} %get-tuple-element.764) | copy-start | bytes 786436 | tf_op jit(solution)/shard_map/while
  112.0 35.7 %copy-start = (bf16[64,2048]{1,0:T(8,128)(2,1)S(1)}, bf16[64,2048]{1,0:T(8,128)(2,1)}, u32[]{:S(2)}) copy-start(bf16[64,2048]{1,0:T(8,128)(2,1)} %get-tuple-element.764) | copy-start | bytes 786436 | tf_op jit(solution)/shard_map/while
  149.1 26.5 %copy-start.1 = (f32[8,4096]{1,0:T(8,128)S(1)}, f32[8,4096]{1,0:T(8,128)}, u32[]{:S(2)}) copy-start(f32[8,4096]{1,0:T(8,128)} %get-tuple-element.887) | copy-start | bytes 393220
  149.4 31.9 %copy-start.4 = (s32[2,64]{1,0:T(2,128)S(1)}, s32[2,64]{1,0:T(2,128)}, u32[]{:S(2)}) copy-start(s32[2,64]{1,0:T(2,128)} %param.27) | copy-start | bytes 1540
  149.4 32.0 %copy-start.2 = (f32[64,256]{1,0:T(8,128)S(1)}, f32[64,256]{1,0:T(8,128)}, u32[]{:S(2)}) copy-start(f32[64,256]{1,0:T(8,128)} %param.25) | copy-start | bytes 196612
  149.5 32.0 %copy-start.3 = (f32[256]{0:T(256)S(1)}, f32[256]{0:T(256)}, u32[]{:S(2)}) copy-start(f32[256]{0:T(256)} %param.24) | copy-start | bytes 3076
  176.7 20.5 %all-to-all-start.1 = ((f32[8,8,4096]{2,1,0:T(8,128)}), f32[8,8,4096]{2,1,0:T(8,128)S(1)}, u32[]{:S(2)}, u32[]{:S(2)}) async-start(f32[8,8,4096]{2,1,0:T(8,128)} %broadcast_in_dim.78), calls=%async_computation.1 | async-start | bytes 2097152 | tf_op jit(solution)/shard_map/all_to_all | solution.py:26
  198.3 22.2 %all-to-all-start.2 = ((f32[16,64,256]{2,1,0:T(8,128)}), f32[16,64,256]{2,1,0:T(8,128)S(1)}, u32[]{:S(2)}, u32[]{:S(2)}) async-start(f32[16,64,256]{2,1,0:T(8,128)} %broadcast_in_dim.79), calls=%async_computation.2 | async-start | bytes 2097152 | tf_op jit(solution)/shard_map/all_to_all | solution.py:26
  221.1 9.9 %copy-start.5 = (f32[8]{0:T(128)S(1)}, f32[8]{0:T(128)}, u32[]{:S(2)}) copy-start(f32[8]{0:T(128)} %param.20) | copy-start | bytes 100
  227.2 24.5 %all-to-all-start.3 = ((f32[8,64,512]{2,1,0:T(8,128)}), f32[8,64,512]{2,1,0:T(8,128)S(1)}, u32[]{:S(2)}, u32[]{:S(2)}) async-start(f32[8,64,512]{2,1,0:T(8,128)} %broadcast_in_dim.80), calls=%async_computation.3 | async-start | bytes 2097152 | tf_op jit(solution)/shard_map/all_to_all | solution.py:26
  290.8 31.8 %all-to-all-start.5 = ((f32[16,64,256]{2,1,0:T(8,128)}), f32[16,64,256]{2,1,0:T(8,128)S(1)}, u32[]{:S(2)}, u32[]{:S(2)}) async-start(f32[16,64,256]{2,1,0:T(8,128)} %broadcast_in_dim.81), calls=%async_computation.5 | async-start | bytes 2097152 | tf_op jit(solution)/shard_map/all_to_all | solution.py:26
  329.3 21.3 %all-to-all-start.6 = ((f32[8,64,512]{2,1,0:T(8,128)}), f32[8,64,512]{2,1,0:T(8,128)S(1)}, u32[]{:S(2)}, u32[]{:S(2)}) async-start(f32[8,64,512]{2,1,0:T(8,128)} %broadcast_in_dim.82), calls=%async_computation.6 | async-start | bytes 2097152 | tf_op jit(solution)/shard_map/all_to_all | solution.py:26
  369.6 21.6 %all-to-all-start.7 = ((f32[16,64,256]{2,1,0:T(8,128)}), f32[16,64,256]{2,1,0:T(8,128)S(1)}, u32[]{:S(2)}, u32[]{:S(2)}) async-start(f32[16,64,256]{2,1,0:T(8,128)} %copy.63), calls=%async_computation.7 | async-start | bytes 2097152 | tf_op jit(solution)/shard_map/all_to_all | solution.py:41
where the time goes:
time: 396 us; the launch traced here: 392 us
  matrix products  188 us (47%)
  waiting for transfers between devices  67.1 us (17%)
  blocking collectives  45.5 us (11%)
  local copies, waits for them, and re-layouts  38.4 us (10%)
  starting transfers between devices  37.5 us (9%)
  other arithmetic  14 us (4%)
    dot_general x4, matrix products, prior_one_block(): lax.dot_general(freq_part, coords, (((0,), (0,)), ((), ())), precision=HI...  143 us
    all_to_all x5, waiting for transfers between devices, sent_to_all(): return lax.all_to_all(copies, axis, split_axis=0, concat_axis=0, tiled=True)  50.5 us
    all_to_all x2, blocking collectives, summed_on_arrival(): lax.all_to_all(pieces, axis, split_axis=0, concat_axis=0, tiled=True)  45.5 us
    all_to_all x5, starting transfers between devices, sent_to_all(): return lax.all_to_all(copies, axis, split_axis=0, concat_axis=0, tiled=True)  33.2 us
    dot_general x4, matrix products, kernel_one_block(): jnp.dot(update, tile, precision=HIGH, preferred_element_type=jnp.float32)  32.5 us
    all_to_all x1, waiting for transfers between devices, summed_on_arrival(): lax.all_to_all(pieces, axis, split_axis=0, concat_axis=0, tiled=True)  16.6 us
    gather x2, local copies, waits for them, and re-layouts, on_device(): row_coords = jnp.take(scaled_all, row_ids, axis=1)  13.6 us
    mul x1, other arithmetic, on_device(): scaled_all = scales[:, None] * all_points  11.3 us
  transfers between devices with their start and end apart: 6, of which 5 were waited for; matrix products, arithmetic and copies ran while one was open for 9% of the time, Pallas kernels for 0%

commit v1 on v0

v1 whole, which is shorter than its diff:
```python
import math

import jax
import jax.numpy as jnp
from jax import lax
from jax.experimental import pallas as pl
from jax.experimental.pallas import tpu as pltpu
from jax.sharding import PartitionSpec as P

F32 = jnp.float32
BF16 = jnp.bfloat16
MESH = pl.DeviceIdType.MESH

D = 8
NW = 16
NN = 8
SAMPLES = 64
GROUP = 128
NGROUPS = 32
PAIRS = 16
KDIM = 64
FHERE = 2048
FCHUNK = 512
ROWS = 512
BCOLS = 1024
NOISE_VAR = 0.1
LN2 = math.log(2.0)
LOG2E = 1.0 / LN2
ROUND = 12582912.0
SIN = (6.283185005, -41.34165573, 81.60100555, -76.54978180, 39.53670502)


def split3(value):
    first = value.astype(BF16).astype(F32)
    rest = value - first
    second = rest.astype(BF16).astype(F32)
    return first, second, rest - second


def rows_of(*rows):
    at = lax.broadcasted_iota(jnp.int32, (8, GROUP), 0)
    result = jnp.zeros((8, GROUP), F32)
    for index, row in enumerate(rows):
        result = jnp.where(at == index, row, result)
    return result


def left_stack(value, extra):
    a, b, c = split3(value)
    return jnp.concatenate([a, a, b, b, a, c, extra, jnp.zeros_like(a)], axis=0)


def right_stack(value, extra):
    a, b, c = split3(value)
    return jnp.concatenate([a, b, a, b, c, a, extra, jnp.zeros_like(a)], axis=0)


def cosine_turns(turns):
    whole = (turns + ROUND) - ROUND
    s = 0.25 - jnp.abs(turns - whole)
    y = s * s
    return s * (SIN[0] + y * (SIN[1] + y * (SIN[2] + y * (SIN[3] + y * SIN[4]))))


def arrange(groups, points, ordered, row_points, place, mine):
    w = lax.axis_index("wide")
    n = lax.axis_index("narrow")

    def group_of(g):
        return points[:, pl.ds(pl.multiple_of(g * GROUP, GROUP), GROUP)]

    member = [lax.rem(groups[k // 8, n * 8 + k % 8], NGROUPS) for k in range(16)]
    for k in range(8):
        row_points[k] = group_of(lax.rem(groups[k // 4, w * 4 + k % 4], NGROUPS))

    @pl.loop(0, NGROUPS)
    def _(g):
        below = jnp.int32(0)
        hits = jnp.int32(0)
        spot = jnp.int32(0)
        for k in range(16):
            below = below + jnp.where(member[k] < g, 1, 0)
            hit = member[k] == g
            hits = hits + jnp.where(hit, 1, 0)
            spot = spot + jnp.where(hit, k, 0)
        at = jnp.where(hits > 0, spot, 16 + g - below)
        place[g] = at
        ordered[at] = group_of(g)
        for i in range(2):
            mine[i, at] = jnp.where(g == 2 * w + i, 1.0, 0.0)


def body(
    place, mine, scales, points, row_points, freq, phases, fw, targets, noise, inverses,
    out, weights,
    amat, bmat, cmat, armat, rows, base, q, h_hi, h_lo, inv_v, inv_hi, inv_lo,
    rs_buf, r_buf, r_hl, wp, nb, wf, w_hl, own, give, cbuf, ubuf, xbuf, vbuf, zbuf,
    inv_sem, wsend, wrecv, nsend, nrecv, rsend, rrecv, fsend, frecv,
):
    w = lax.axis_index("wide")
    n = lax.axis_index("narrow")
    core = lax.rem(w, 2)
    x_here = lax.rem(lax.div(w, 2), 4)
    z_here = lax.div(w, 8)

    def wide_dev(peer):
        return {"wide": peer}

    def narrow_dev(peer):
        return {"narrow": peer}

    barrier = pltpu.get_barrier_semaphore()

    @pl.loop(1, NW)
    def _(d):
        pl.semaphore_signal(barrier, inc=1, device_id=wide_dev(lax.rem(w + d, NW)), device_id_type=MESH)

    @pl.loop(1, NN)
    def _(d):
        pl.semaphore_signal(barrier, inc=1, device_id=narrow_dev(lax.rem(n + d, NN)), device_id_type=MESH)

    inv_copy = pltpu.make_async_copy(inverses, inv_v, inv_sem)
    inv_copy.start()

    scale_col = jnp.concatenate([jnp.full((1, GROUP), scales[d], F32) for d in range(D)], axis=0)
    coord_scale = scale_col * (math.sqrt(5.0) * LOG2E)
    ones = jnp.ones((1, GROUP), F32)

    @pl.loop(0, FHERE // GROUP)
    def _(k):
        at = pl.ds(pl.multiple_of(k * GROUP, GROUP), GROUP)
        f = freq[:, at] * (0.5 / math.pi)
        ph = split3(phases[:, at] * (0.5 / math.pi))
        amat[at, :] = left_stack(f, rows_of(*ph)).T.astype(BF16)

    @pl.loop(0, NGROUPS)
    def _(g):
        pts = points[g]
        bmat[g] = right_stack(pts, rows_of(ones, ones, ones)).astype(BF16)
        z = (pts - 0.5) * coord_scale
        t = split3(jnp.sum(z * z, axis=0, keepdims=True))
        cmat[g] = right_stack(z, rows_of(ones, ones, ones, *t)).astype(BF16)

    for i in range(2):
        at = slice(i * GROUP, (i + 1) * GROUP)
        base[i] = targets[:, at] - noise[:, at]

    def prior_pairs(lo, hi):
        @pl.loop(lo, hi)
        def _(pair):
            rhs = jnp.concatenate([bmat[2 * pair], bmat[2 * pair + 1]], axis=1)
            acc = jnp.zeros((SAMPLES, 2 * GROUP), F32)
            for k in range(FHERE // FCHUNK):
                at = slice(k * FCHUNK, (k + 1) * FCHUNK)
                turns = jnp.dot(amat[at, :], rhs, preferred_element_type=F32)
                features = cosine_turns(turns).astype(BF16)
                acc = acc + jnp.dot(fw[:, at], features, preferred_element_type=F32)
            for i in range(2):
                at = 2 * pair + i
                own_base = mine[0, at] * base[0] + mine[1, at] * base[1]
                q[at] = own_base - acc[:, i * GROUP : (i + 1) * GROUP] * (1.0 / 128.0)

    def kernel_pairs(lo, hi):
        @pl.loop(lo, hi)
        def _(pair):
            rhs = jnp.concatenate([cmat[2 * pair], cmat[2 * pair + 1]], axis=1)
            for b in range(2):
                for k in range(2):
                    at = slice(k * 256, (k + 1) * 256)
                    m = jnp.dot(armat[b, at, :], rhs, preferred_element_type=F32)
                    m = jnp.maximum(m, 1e-12)
                    u = m * lax.rsqrt(m)
                    h = (1.0 + u * LN2 + m * (LN2 * LN2 / 3.0)) * jnp.exp2(-u)
                    hi_part = h.astype(BF16)
                    h_hi[b, pair, at, :] = hi_part
                    h_lo[b, pair, at, :] = (h - hi_part.astype(F32)).astype(BF16)

    def wide_chunk(ref, peer):
        return ref.at[lax.div(peer, 2), pl.ds(pl.multiple_of(lax.rem(peer, 2) * 32, 32), 32)]

    def wide_copy(b, phase, d, gather):
        peer = lax.rem(w + d, NW)
        k = 2 * b + phase
        if gather:
            src = wide_chunk(r_buf.at[b], w)
            dst = wide_chunk(r_buf.at[b], w)
        else:
            src = wide_chunk(q.at[pl.ds(8 * b, 8)], peer)
            dst = rs_buf.at[b, d - 1]
        return pltpu.make_async_remote_copy(
            src_ref=src, dst_ref=dst, send_sem=wsend.at[k, d], recv_sem=wrecv.at[k, d],
            device_id=wide_dev(peer), device_id_type=MESH,
        )

    def wide_arrival(b, phase, d, gather):
        peer = lax.rem(w + NW - d, NW)
        k = 2 * b + phase
        dst = wide_chunk(r_buf.at[b], peer) if gather else rs_buf.at[b, d - 1]
        return pltpu.make_async_remote_copy(
            src_ref=dst, dst_ref=dst, send_sem=wsend.at[k, d], recv_sem=wrecv.at[k, d],
            device_id=wide_dev(peer), device_id_type=MESH,
        )

    def start_wide(b, gather):
        @pl.loop(1, NW)
        def _(d):
            wide_copy(b, int(gather), d, gather).start()

    def end_wide(b, gather):
        @pl.loop(1, NW)
        def _(d):
            wide_arrival(b, int(gather), d, gather).wait_recv()

    def end_sends(b):
        @pl.loop(1, NW)
        def _(d):
            wide_copy(b, 0, d, False).wait_send()

    def sum_wide(b):
        total = wide_chunk(q.at[pl.ds(8 * b, 8)], w)[...]
        for d in range(NW - 1):
            total = total + rs_buf[b, d]
        wide_chunk(r_buf.at[b], w)[...] = total

    def narrow_copy(b, phase, d):
        peer = lax.rem(n + d, NN)
        k = 2 * b + phase
        mine = pl.ds(pl.multiple_of(n * 8, 8), 8)
        theirs = pl.ds(pl.multiple_of(peer * 8, 8), 8)
        if phase:
            src, dst = wf.at[b, mine], wf.at[b, mine]
        else:
            src, dst = wp.at[b, theirs], nb.at[b, d - 1]
        return pltpu.make_async_remote_copy(
            src_ref=src, dst_ref=dst, send_sem=nsend.at[k, d], recv_sem=nrecv.at[k, d],
            device_id=narrow_dev(peer), device_id_type=MESH,
        )

    def narrow_arrival(b, phase, d):
        peer = lax.rem(n + NN - d, NN)
        k = 2 * b + phase
        theirs = pl.ds(pl.multiple_of(peer * 8, 8), 8)
        dst = wf.at[b, theirs] if phase else nb.at[b, d - 1]
        return pltpu.make_async_remote_copy(
            src_ref=dst, dst_ref=dst, send_sem=nsend.at[k, d], recv_sem=nrecv.at[k, d],
            device_id=narrow_dev(peer), device_id_type=MESH,
        )

    def start_narrow(b, phase):
        @pl.loop(1, NN)
        def _(d):
            narrow_copy(b, phase, d).start()

    def end_narrow(b, phase):
        @pl.loop(1, NN)
        def _(d):
            narrow_arrival(b, phase, d).wait_recv()

    def sum_narrow(b):
        mine = pl.ds(pl.multiple_of(n * 8, 8), 8)
        total = wp[b, mine]
        for d in range(NN - 1):
            total = total + nb[b, d]
        wf[b, mine] = total

    def solve(b):
        for k in range(8):
            at = slice(k * GROUP, (k + 1) * GROUP)
            value = r_buf[b, k]
            hi_part = value.astype(BF16)
            r_hl[0:SAMPLES, at] = hi_part
            r_hl[SAMPLES:, at] = (value - hi_part.astype(F32)).astype(BF16)
        dims = (((1,), (1,)), ((), ()))
        both = lax.dot_general(r_hl[...], inv_hi[b], dims, preferred_element_type=F32)
        low = lax.dot_general(r_hl[0:SAMPLES, :], inv_lo[b], dims, preferred_element_type=F32)
        wp[b] = both[:SAMPLES] + both[SAMPLES:] + low

    def finish_weights(b):
        value = wf[b]
        weights[b] = value
        hi_part = value.astype(BF16)
        w_hl[b, 0:SAMPLES, :] = hi_part
        w_hl[b, SAMPLES:, :] = (value - hi_part.astype(F32)).astype(BF16)

    def apply_pairs(b, lo, hi):
        @pl.loop(lo, hi)
        def _(pair):
            both = jnp.dot(w_hl[b], h_hi[b, pair], preferred_element_type=F32)
            low = jnp.dot(w_hl[b, 0:SAMPLES, :], h_lo[b, pair], preferred_element_type=F32)
            total = both[:SAMPLES] + both[SAMPLES:] + low
            for i in range(2):
                q[2 * pair + i] = q[2 * pair + i] - total[:, i * GROUP : (i + 1) * GROUP]

    def apply_noise(b):
        @pl.when(n == lax.div(w, 2))
        def _():
            for k in range(4):
                at = 8 * b + lax.rem(w, 2) * 4 + k
                q[at] = q[at] - NOISE_VAR * wf[b, :, k * GROUP : (k + 1) * GROUP]

    def rows_copy(d):
        return pltpu.make_async_remote_copy(
            src_ref=rows, dst_ref=rows, send_sem=rsend.at[d], recv_sem=rrecv.at[0],
            device_id=narrow_dev(lax.rem(n + d, NN)), device_id_type=MESH,
        )

    prior_pairs(0, 4)
    pl.semaphore_wait(barrier, NW - 1 + NN - 1)
    start_wide(0, False)
    holder = n == lax.div(w, 2)

    @pl.when(holder)
    def _():
        rows[...] = row_points[...]

        @pl.loop(1, NN)
        def _(d):
            rows_copy(d).start()

    prior_pairs(4, 8)
    end_wide(0, False)
    sum_wide(0)
    start_wide(0, True)

    @pl.when(jnp.logical_not(holder))
    def _():
        pltpu.make_async_remote_copy(
            src_ref=rows, dst_ref=rows, send_sem=rsend.at[0], recv_sem=rrecv.at[0],
            device_id=narrow_dev(lax.rem(n + 1, NN)), device_id_type=MESH,
        ).wait_recv()

    for k in range(8):
        z = (rows[k] - 0.5) * coord_scale
        t = split3(jnp.sum(z * z, axis=0, keepdims=True))
        stack = left_stack(-2.0 * z, rows_of(*t, ones, ones, ones))
        armat[k // 4, (k % 4) * GROUP : (k % 4 + 1) * GROUP, :] = stack.T.astype(BF16)

    inv_copy.wait()

    @pl.loop(0, 2 * ROWS // 64)
    def _(i):
        b = lax.div(i, ROWS // 64)
        at = pl.ds(pl.multiple_of(lax.rem(i, ROWS // 64) * 64, 64), 64)
        value = inv_v[b, at, :]
        hi_part = value.astype(BF16)
        inv_hi[b, at, :] = hi_part
        inv_lo[b, at, :] = (value - hi_part.astype(F32)).astype(BF16)

    kernel_pairs(4, 8)
    prior_pairs(8, 10)
    end_wide(0, True)
    solve(0)
    start_narrow(0, 0)
    prior_pairs(10, 12)
    end_narrow(0, 0)
    sum_narrow(0)
    start_narrow(0, 1)
    prior_pairs(12, 14)
    end_narrow(0, 1)
    finish_weights(0)
    apply_pairs(0, 4, 8)
    start_wide(1, False)
    prior_pairs(14, 16)
    kernel_pairs(0, 4)
    end_wide(1, False)
    sum_wide(1)
    start_wide(1, True)
    kernel_pairs(8, 16)
    end_wide(1, True)
    solve(1)
    start_narrow(1, 0)
    end_sends(0)
    apply_pairs(0, 0, 4)
    apply_noise(0)
    apply_pairs(0, 8, 16)
    end_narrow(1, 0)
    sum_narrow(1)
    start_narrow(1, 1)
    end_narrow(1, 1)
    finish_weights(1)

    end_sends(1)
    apply_pairs(1, 0, 16)
    apply_noise(1)

    for x in range(4):
        for z in range(2):
            for i in range(2):
                own[x, z, i] = q[place[2 * (z * 8 + x * 2 + core) + i]]
                give[x, z, i] = q[place[2 * (z * 8 + x * 2 + 1 - core) + i]]

    core_copy = pltpu.make_async_remote_copy(
        src_ref=give, dst_ref=cbuf, send_sem=fsend.at[0], recv_sem=frecv.at[0],
        device_id=wide_dev(w + 1 - 2 * core), device_id_type=MESH,
    )
    core_copy.start()
    core_copy.wait_recv()
    for x in range(4):
        ubuf[x] = own[x] + cbuf[x]

    def x_copy(d):
        peer = lax.rem(x_here + d, 4)
        return pltpu.make_async_remote_copy(
            src_ref=ubuf.at[peer], dst_ref=xbuf.at[d - 1], send_sem=fsend.at[d], recv_sem=frecv.at[d],
            device_id=wide_dev(z_here * 8 + peer * 2 + core), device_id_type=MESH,
        )

    for d in range(1, 4):
        x_copy(d).start()
    for d in range(1, 4):
        x_copy(d).wait_recv()
    vbuf[...] = ubuf[x_here] + xbuf[0] + xbuf[1] + xbuf[2]
    z_copy = pltpu.make_async_remote_copy(
        src_ref=vbuf.at[1 - z_here], dst_ref=zbuf, send_sem=fsend.at[4], recv_sem=frecv.at[4],
        device_id=wide_dev((1 - z_here) * 8 + x_here * 2 + core), device_id_type=MESH,
    )
    z_copy.start()
    z_copy.wait_recv()
    total = vbuf[z_here] + zbuf[...]
    for i in range(2):
        out[:, i * GROUP : (i + 1) * GROUP] = total[i]

    @pl.loop(1, NW)
    def _(d):
        wide_copy(0, 1, d, True).wait_send()
        wide_copy(1, 1, d, True).wait_send()

    @pl.loop(1, NN)
    def _(d):
        for b in range(2):
            for phase in range(2):
                narrow_copy(b, phase, d).wait_send()

    @pl.when(holder)
    def _():
        @pl.loop(1, NN)
        def _(d):
            rows_copy(d).wait_send()

    core_copy.wait_send()
    for d in range(1, 4):
        x_copy(d).wait_send()
    z_copy.wait_send()


def on_device(points, scales, frequencies, phases, feature_weights, targets, noise, inverses, groups):
    vmem = pl.BlockSpec(memory_space=pltpu.VMEM)
    smem = pl.BlockSpec(memory_space=pltpu.SMEM)
    tile = (SAMPLES, GROUP)
    dma = pltpu.SemaphoreType.DMA
    ordered, row_points, place, mine = pl.pallas_call(
        arrange,
        out_shape=(
            jax.ShapeDtypeStruct((NGROUPS, D, GROUP), F32),
            jax.ShapeDtypeStruct((8, D, GROUP), F32),
            jax.ShapeDtypeStruct((NGROUPS,), jnp.int32),
            jax.ShapeDtypeStruct((2, NGROUPS), F32),
        ),
        in_specs=[smem, vmem],
        out_specs=(vmem, vmem, smem, smem),
        name="arrange",
    )(groups, points)
    return pl.pallas_call(
        body,
        out_shape=(
            jax.ShapeDtypeStruct((SAMPLES, 2 * GROUP), F32),
            jax.ShapeDtypeStruct((2, SAMPLES, ROWS), F32),
        ),
        in_specs=[smem, smem, smem] + [vmem] * 7 + [pl.BlockSpec(memory_space=pl.ANY)],
        out_specs=(vmem, vmem),
        scratch_shapes=[
            pltpu.VMEM((FHERE, KDIM), BF16),
            pltpu.VMEM((NGROUPS, KDIM, GROUP), BF16),
            pltpu.VMEM((NGROUPS, KDIM, GROUP), BF16),
            pltpu.VMEM((2, ROWS, KDIM), BF16),
            pltpu.VMEM((8, D, GROUP), F32),
            pltpu.VMEM((2, *tile), F32),
            pltpu.VMEM((NGROUPS, *tile), F32),
            pltpu.VMEM((2, PAIRS, ROWS, 2 * GROUP), BF16),
            pltpu.VMEM((2, PAIRS, ROWS, 2 * GROUP), BF16),
            pltpu.VMEM((2, ROWS, BCOLS), F32),
            pltpu.VMEM((2, ROWS, BCOLS), BF16),
            pltpu.VMEM((2, ROWS, BCOLS), BF16),
            pltpu.VMEM((2, NW - 1, 32, GROUP), F32),
            pltpu.VMEM((2, 8, *tile), F32),
            pltpu.VMEM((2 * SAMPLES, BCOLS), BF16),
            pltpu.VMEM((2, SAMPLES, ROWS), F32),
            pltpu.VMEM((2, NN - 1, 8, ROWS), F32),
            pltpu.VMEM((2, SAMPLES, ROWS), F32),
            pltpu.VMEM((2, 2 * SAMPLES, ROWS), BF16),
            pltpu.VMEM((4, 2, 2, *tile), F32),
            pltpu.VMEM((4, 2, 2, *tile), F32),
            pltpu.VMEM((4, 2, 2, *tile), F32),
            pltpu.VMEM((4, 2, 2, *tile), F32),
            pltpu.VMEM((3, 2, 2, *tile), F32),
            pltpu.VMEM((2, 2, *tile), F32),
            pltpu.VMEM((2, *tile), F32),
            dma,
            dma((4, NW)),
            dma((4, NW)),
            dma((4, NN)),
            dma((4, NN)),
            dma((NN,)),
            dma((1,)),
            dma((5,)),
            dma((5,)),
        ],
        compiler_params=pltpu.CompilerParams(collective_id=0, has_side_effects=True),
        name="posterior",
    )(
        place, mine, scales, ordered, row_points, frequencies, phases.reshape(1, -1), feature_weights,
        targets.reshape(1, -1), noise, inverses,
    )


def solution(mesh):
    in_specs = (
        P(None, "narrow"),
        P(),
        P(None, "wide"),
        P("wide"),
        P(None, "wide"),
        P(("narrow", "wide")),
        P(None, ("narrow", "wide")),
        P(None, "wide", "narrow"),
        P(),
    )
    out_specs = (P(None, ("narrow", "wide")), P(None, None, "wide"))
    return jax.shard_map(on_device, mesh=mesh, in_specs=in_specs, out_specs=out_specs, check_vma=False)
```

time: 396 us -> 85.1 us (0.21)
  matrix products: 188 us -> 0 us
  Pallas kernels: 0 us -> 81.1 us
  waiting for transfers between devices: 67.1 us -> 0 us
  blocking collectives: 45.5 us -> 0 us
  starting transfers between devices: 37.5 us -> 0 us
  local copies, waits for them, and re-layouts: 38.4 us -> 3.14 us
  other arithmetic: 14 us -> 0 us
    dot_general x14 -> x0, matrix products: 188 us -> none  [the longest x4 143 us: prior_one_block(): lax.dot_general(freq_part, coords, (((0,), (0,)), ((), ())), precision=HI...]
    pallas_call x0 -> x2, Pallas kernels: none -> 81.1 us  [the longest x1 77.5 us: on_device(): pl.pallas_call(body, out_shape=(jax.ShapeDtypeStruct((SAMPLES, 2 * GROUP)...]
    all_to_all x6 -> x0, waiting for transfers between devices: 67.1 us -> none  [the longest x5 50.5 us: sent_to_all(): return lax.all_to_all(copies, axis, split_axis=0, concat_axis=0, tiled=True)]
    all_to_all x2 -> x0, blocking collectives: 45.5 us -> none  [summed_on_arrival(): lax.all_to_all(pieces, axis, split_axis=0, concat_axis=0, tiled=True)]
    all_to_all x6 -> x0, starting transfers between devices: 37.5 us -> none  [the longest x5 33.2 us: sent_to_all(): return lax.all_to_all(copies, axis, split_axis=0, concat_axis=0, tiled=True)]
    gather x4 -> x0, local copies, waits for them, and re-layouts: 14.7 us -> none  [the longest x2 13.6 us: on_device(): row_coords = jnp.take(scaled_all, row_ids, axis=1)]
    transpose x6 -> x0, local copies, waits for them, and re-layouts: 12.3 us -> none  [the longest x3 9.44 us: laid_out(): pieces = jnp.moveaxis(pieces, 0, dim)]
    mul x3 -> x0, other arithmetic: 11.4 us -> none  [the longest x1 11.3 us: on_device(): scaled_all = scales[:, None] * all_points]
  transfers between devices with their start and end apart: 6 -> 0, of which waited for: 5 -> 0; matrix products, arithmetic and copies ran while one was open for 9% -> 0% of each run, Pallas kernels for 0% -> 0%
where the time goes in v1:
time: 85.1 us; the launch traced here: 84.9 us
  Pallas kernels  81.1 us (95%)
  local copies, waits for them, and re-layouts  3.14 us (4%)
    pallas_call x1, Pallas kernels, on_device(): pl.pallas_call(body, out_shape=(jax.ShapeDtypeStruct((SAMPLES, 2 * GROUP)...  77.5 us
    pallas_call x1, Pallas kernels, on_device(): pl.pallas_call(arrange, out_shape=(jax.ShapeDtypeStruct((NGROUPS, D, GROU...  3.61 us
    unnamed x2, local copies, waits for them, and re-layouts  3.14 us

profile of v1, /device:TPU:1, one launch (start us, length us, event | category | flops | bytes accessed | tf_op | source)
XLA Modules:
  0.0 84.9 jit_solution(16040637763826707711)
XLA Ops:
  0.6 3.6 %arrange.1 = (f32[32,8,128]{2,1,0:T(8,128)}, f32[8,8,128]{2,1,0:T(8,128)}, s32[32]{0:T(128)}, f32[2,32]{1,0:T(2,128)}) custom-call(s32[2,64]{1,0:T(2,128)} %groups.1, f32[8,4096]{1,0:T(8,128)} %points.1), custom_call_target="tpu_custom_call" | custom-call | tf_op jit(solution)/shard_map/arrange/pallas_call | solution.py:451
  4.2 77.5 %posterior.1 = (f32[64,256]{1,0:T(8,128)}, f32[2,64,512]{2,1,0:T(8,128)}) custom-call(s32[32]{0:T(128)} %get-tuple-element.6.place, f32[2,32]{1,0:T(2,128)} %get-tuple-element.7.mine, f32[8]{0:T(128)} %scales.1, f32[32,8,128]{2,1,0:T(8,128)} %get-tuple-element.8.points, f32[8,8,128]{2,1,0:T(8,128)} %get-tuple-element.9.row_points, f32[8,2048]{1,0:T(8,128)} %freq.1, ...), custom_call_target="tpu_custom_call" | custom-call | tf_op jit(solution)/shard_map/posterior/pallas_call | solution.py:463
  81.8 1.5 %copy.13 = f32[64,256]{1,0:T(8,128)} copy(f32[64,256]{1,0:T(8,128)} %get-tuple-element.12) | data formatting | bytes 131072
  83.2 1.7 %copy.14 = f32[2,64,512]{2,1,0:T(8,128)} copy(f32[2,64,512]{2,1,0:T(8,128)} %get-tuple-element.13) | data formatting | bytes 524288

commit v2 on v1

--- a/solution.py
+++ b/solution.py
@@ -62,40 +62,37 @@
     return s * (SIN[0] + y * (SIN[1] + y * (SIN[2] + y * (SIN[3] + y * SIN[4]))))
 
 
-def arrange(groups, points, ordered, row_points, place, mine):
+def arrange(groups, order, place, mine):
     w = lax.axis_index("wide")
     n = lax.axis_index("narrow")
-
-    def group_of(g):
-        return points[:, pl.ds(pl.multiple_of(g * GROUP, GROUP), GROUP)]
-
-    member = [lax.rem(groups[k // 8, n * 8 + k % 8], NGROUPS) for k in range(16)]
+    for g in range(NGROUPS):
+        place[g] = -1
+    for g in range(2 * NGROUPS):
+        mine[g] = 0.0
+    for k in range(16):
+        g = lax.rem(groups[k // 8, n * 8 + k % 8], NGROUPS)
+        order[k] = g
+        place[g] = k
     for k in range(8):
-        row_points[k] = group_of(lax.rem(groups[k // 4, w * 4 + k % 4], NGROUPS))
-
-    @pl.loop(0, NGROUPS)
-    def _(g):
-        below = jnp.int32(0)
-        hits = jnp.int32(0)
-        spot = jnp.int32(0)
-        for k in range(16):
-            below = below + jnp.where(member[k] < g, 1, 0)
-            hit = member[k] == g
-            hits = hits + jnp.where(hit, 1, 0)
-            spot = spot + jnp.where(hit, k, 0)
-        at = jnp.where(hits > 0, spot, 16 + g - below)
+        order[NGROUPS + k] = lax.rem(groups[k // 4, w * 4 + k % 4], NGROUPS)
+    count = jnp.int32(16)
+    for g in range(NGROUPS):
+        at = place[g]
+        free = at < 0
+        at = jnp.where(free, count, at)
         place[g] = at
-        ordered[at] = group_of(g)
-        for i in range(2):
-            mine[i, at] = jnp.where(g == 2 * w + i, 1.0, 0.0)
+        order[at] = g
+        count = count + jnp.where(free, 1, 0)
+    for i in range(2):
+        mine[i * NGROUPS + place[2 * w + i]] = 1.0
 
 
 def body(
-    place, mine, scales, points, row_points, freq, phases, fw, targets, noise, inverses,
-    out, weights,
+    order, place, mine, scales, points, freq, phases, fw, targets, noise, inverses,
+    result,
     amat, bmat, cmat, armat, rows, base, q, h_hi, h_lo, inv_v, inv_hi, inv_lo,
-    rs_buf, r_buf, r_hl, wp, nb, wf, w_hl, own, give, cbuf, ubuf, xbuf, vbuf, zbuf,
-    inv_sem, wsend, wrecv, nsend, nrecv, rsend, rrecv, fsend, frecv,
+    rs_buf, r_buf, r_hl, wp, nb, wf, w_hl, own, give, cbuf, fbuf, pts,
+    inv_sem, wsend, wrecv, nsend, nrecv, rsend, rrecv, csend, crecv, fsend, frecv,
 ):
     w = lax.axis_index("wide")
     n = lax.axis_index("narrow")
@@ -135,9 +132,11 @@
 
     @pl.loop(0, NGROUPS)
     def _(g):
-        pts = points[g]
-        bmat[g] = right_stack(pts, rows_of(ones, ones, ones)).astype(BF16)
-        z = (pts - 0.5) * coord_scale
+        at = pl.ds(pl.multiple_of(g * GROUP, GROUP), GROUP)
+        here = points[:, at]
+        pts[g] = here
+        bmat[g] = right_stack(here, rows_of(ones, ones, ones)).astype(BF16)
+        z = (here - 0.5) * coord_scale
         t = split3(jnp.sum(z * z, axis=0, keepdims=True))
         cmat[g] = right_stack(z, rows_of(ones, ones, ones, *t)).astype(BF16)
 
@@ -148,7 +147,7 @@
     def prior_pairs(lo, hi):
         @pl.loop(lo, hi)
         def _(pair):
-            rhs = jnp.concatenate([bmat[2 * pair], bmat[2 * pair + 1]], axis=1)
+            rhs = jnp.concatenate([bmat[order[2 * pair]], bmat[order[2 * pair + 1]]], axis=1)
             acc = jnp.zeros((SAMPLES, 2 * GROUP), F32)
             for k in range(FHERE // FCHUNK):
                 at = slice(k * FCHUNK, (k + 1) * FCHUNK)
@@ -157,13 +156,13 @@
                 acc = acc + jnp.dot(fw[:, at], features, preferred_element_type=F32)
             for i in range(2):
                 at = 2 * pair + i
-                own_base = mine[0, at] * base[0] + mine[1, at] * base[1]
+                own_base = mine[at] * base[0] + mine[NGROUPS + at] * base[1]
                 q[at] = own_base - acc[:, i * GROUP : (i + 1) * GROUP] * (1.0 / 128.0)
 
     def kernel_pairs(lo, hi):
         @pl.loop(lo, hi)
         def _(pair):
-            rhs = jnp.concatenate([cmat[2 * pair], cmat[2 * pair + 1]], axis=1)
+            rhs = jnp.concatenate([cmat[order[2 * pair]], cmat[order[2 * pair + 1]]], axis=1)
             for b in range(2):
                 for k in range(2):
                     at = slice(k * 256, (k + 1) * 256)
@@ -172,8 +171,11 @@
                     u = m * lax.rsqrt(m)
                     h = (1.0 + u * LN2 + m * (LN2 * LN2 / 3.0)) * jnp.exp2(-u)
                     hi_part = h.astype(BF16)
-                    h_hi[b, pair, at, :] = hi_part
-                    h_lo[b, pair, at, :] = (h - hi_part.astype(F32)).astype(BF16)
+                    lo_part = (h - hi_part.astype(F32)).astype(BF16)
+                    for i in range(2):
+                        half = slice(i * GROUP, (i + 1) * GROUP)
+                        h_hi[b, 2 * pair + i, at, :] = hi_part[:, half]
+                        h_lo[b, 2 * pair + i, at, :] = lo_part[:, half]
 
     def wide_chunk(ref, peer):
         return ref.at[lax.div(peer, 2), pl.ds(pl.multiple_of(lax.rem(peer, 2) * 32, 32), 32)]
@@ -277,17 +279,22 @@
 
     def finish_weights(b):
         value = wf[b]
-        weights[b] = value
+        result[:, 2 * GROUP + b * ROWS : 2 * GROUP + (b + 1) * ROWS] = value
         hi_part = value.astype(BF16)
         w_hl[b, 0:SAMPLES, :] = hi_part
         w_hl[b, SAMPLES:, :] = (value - hi_part.astype(F32)).astype(BF16)
 
+    def change(b, p0, p1):
+        hi_tile = jnp.concatenate([h_hi[b, p0], h_hi[b, p1]], axis=1)
+        lo_tile = jnp.concatenate([h_lo[b, p0], h_lo[b, p1]], axis=1)
+        both = jnp.dot(w_hl[b], hi_tile, preferred_element_type=F32)
+        low = jnp.dot(w_hl[b, 0:SAMPLES, :], lo_tile, preferred_element_type=F32)
+        return both[:SAMPLES] + both[SAMPLES:] + low
+
     def apply_pairs(b, lo, hi):
         @pl.loop(lo, hi)
         def _(pair):
-            both = jnp.dot(w_hl[b], h_hi[b, pair], preferred_element_type=F32)
-            low = jnp.dot(w_hl[b, 0:SAMPLES, :], h_lo[b, pair], preferred_element_type=F32)
-            total = both[:SAMPLES] + both[SAMPLES:] + low
+            total = change(b, 2 * pair, 2 * pair + 1)
             for i in range(2):
                 q[2 * pair + i] = q[2 * pair + i] - total[:, i * GROUP : (i + 1) * GROUP]
 
@@ -311,7 +318,8 @@
 
     @pl.when(holder)
     def _():
-        rows[...] = row_points[...]
+        for k in range(8):
+            rows[k] = pts[order[NGROUPS + k]]
 
         @pl.loop(1, NN)
         def _(d):
@@ -380,45 +388,53 @@
     finish_weights(1)
 
     end_sends(1)
-    apply_pairs(1, 0, 16)
     apply_noise(1)
 
-    for x in range(4):
-        for z in range(2):
-            for i in range(2):
-                own[x, z, i] = q[place[2 * (z * 8 + x * 2 + core) + i]]
-                give[x, z, i] = q[place[2 * (z * 8 + x * 2 + 1 - core) + i]]
-
-    core_copy = pltpu.make_async_remote_copy(
-        src_ref=give, dst_ref=cbuf, send_sem=fsend.at[0], recv_sem=frecv.at[0],
-        device_id=wide_dev(w + 1 - 2 * core), device_id_type=MESH,
-    )
-    core_copy.start()
-    core_copy.wait_recv()
-    for x in range(4):
-        ubuf[x] = own[x] + cbuf[x]
-
-    def x_copy(d):
-        peer = lax.rem(x_here + d, 4)
-        return pltpu.make_async_remote_copy(
-            src_ref=ubuf.at[peer], dst_ref=xbuf.at[d - 1], send_sem=fsend.at[d], recv_sem=frecv.at[d],
-            device_id=wide_dev(z_here * 8 + peer * 2 + core), device_id_type=MESH,
-        )
-
-    for d in range(1, 4):
-        x_copy(d).start()
-    for d in range(1, 4):
-        x_copy(d).wait_recv()
-    vbuf[...] = ubuf[x_here] + xbuf[0] + xbuf[1] + xbuf[2]
-    z_copy = pltpu.make_async_remote_copy(
-        src_ref=vbuf.at[1 - z_here], dst_ref=zbuf, send_sem=fsend.at[4], recv_sem=frecv.at[4],
-        device_id=wide_dev((1 - z_here) * 8 + x_here * 2 + core), device_id_type=MESH,
-    )
-    z_copy.start()
-    z_copy.wait_recv()
-    total = vbuf[z_here] + zbuf[...]
+    def chip(rel):
+        return lax.rem(z_here + lax.div(rel, 4), 2) * 8 + lax.rem(x_here + lax.rem(rel, 4), 4) * 2
+
+    def final_piece(dest):
+        p0, p1 = place[2 * dest], place[2 * dest + 1]
+        total = change(1, p0, p1)
+        return q[p0] - total[:, :GROUP], q[p1] - total[:, GROUP:]
+
+    def core_copy(rel):
+        return pltpu.make_async_remote_copy(
+            src_ref=give.at[rel], dst_ref=cbuf.at[rel], send_sem=csend.at[rel], recv_sem=crecv.at[rel],
+            device_id=wide_dev(w + 1 - 2 * core), device_id_type=MESH,
+        )
+
+    def chip_copy(rel):
+        return pltpu.make_async_remote_copy(
+            src_ref=own.at[rel], dst_ref=fbuf.at[rel - 1], send_sem=fsend.at[rel], recv_sem=frecv.at[rel],
+            device_id=wide_dev(chip(rel) + core), device_id_type=MESH,
+        )
+
+    @pl.loop(0, 8)
+    def _(j):
+        rel = 7 - j
+        piece = final_piece(chip(rel) + 1 - core)
+        for i in range(2):
+            give[rel, i] = piece[i]
+        core_copy(rel).start()
+
+    @pl.loop(0, 7)
+    def _(j):
+        rel = 7 - j
+        piece = final_piece(chip(rel) + core)
+        core_copy(rel).wait_recv()
+        for i in range(2):
+            own[rel, i] = piece[i] + cbuf[rel, i]
+        chip_copy(rel).start()
+
+    piece = final_piece(w)
+    core_copy(0).wait_recv()
+    total = [piece[i] + cbuf[0, i] for i in range(2)]
+    for rel in range(7, 0, -1):
+        chip_copy(rel).wait_recv()
+        total = [total[i] + fbuf[rel - 1, i] for i in range(2)]
     for i in range(2):
-        out[:, i * GROUP : (i + 1) * GROUP] = total[i]
+        result[:, i * GROUP : (i + 1) * GROUP] = total[i]
 
     @pl.loop(1, NW)
     def _(d):
@@ -437,10 +453,19 @@
         def _(d):
             rows_copy(d).wait_send()
 
-    core_copy.wait_send()
-    for d in range(1, 4):
-        x_copy(d).wait_send()
-    z_copy.wait_send()
+    @pl.loop(0, 8)
+    def _(rel):
+        core_copy(rel).wait_send()
+
+    @pl.loop(1, 8)
+    def _(rel):
+        chip_copy(rel).wait_send()
+
+
+def unpack(result, residual, weights):
+    residual[...] = result[:, : 2 * GROUP]
+    for b in range(2):
+        weights[b] = result[:, 2 * GROUP + b * ROWS : 2 * GROUP + (b + 1) * ROWS]
 
 
 def on_device(points, scales, frequencies, phases, feature_weights, targets, noise, inverses, groups):
@@ -448,26 +473,22 @@
     smem = pl.BlockSpec(memory_space=pltpu.SMEM)
     tile = (SAMPLES, GROUP)
     dma = pltpu.SemaphoreType.DMA
-    ordered, row_points, place, mine = pl.pallas_call(
+    order, place, mine = pl.pallas_call(
         arrange,
         out_shape=(
-            jax.ShapeDtypeStruct((NGROUPS, D, GROUP), F32),
-            jax.ShapeDtypeStruct((8, D, GROUP), F32),
+            jax.ShapeDtypeStruct((NGROUPS + 8,), jnp.int32),
             jax.ShapeDtypeStruct((NGROUPS,), jnp.int32),
-            jax.ShapeDtypeStruct((2, NGROUPS), F32),
+            jax.ShapeDtypeStruct((2 * NGROUPS,), F32),
         ),
-        in_specs=[smem, vmem],
-        out_specs=(vmem, vmem, smem, smem),
+        in_specs=[smem],
+        out_specs=(smem, smem, smem),
         name="arrange",
-    )(groups, points)
-    return pl.pallas_call(
+    )(groups)
+    result = pl.pallas_call(
         body,
-        out_shape=(
-            jax.ShapeDtypeStruct((SAMPLES, 2 * GROUP), F32),
-            jax.ShapeDtypeStruct((2, SAMPLES, ROWS), F32),
-        ),
-        in_specs=[smem, smem, smem] + [vmem] * 7 + [pl.BlockSpec(memory_space=pl.ANY)],
-        out_specs=(vmem, vmem),
+        out_shape=jax.ShapeDtypeStruct((SAMPLES, 2 * GROUP + 2 * ROWS), F32),
+        in_specs=[smem] * 4 + [vmem] * 6 + [pl.BlockSpec(memory_space=pl.ANY)],
+        out_specs=vmem,
         scratch_shapes=[
             pltpu.VMEM((FHERE, KDIM), BF16),
             pltpu.VMEM((NGROUPS, KDIM, GROUP), BF16),
@@ -476,8 +497,8 @@
             pltpu.VMEM((8, D, GROUP), F32),
             pltpu.VMEM((2, *tile), F32),
             pltpu.VMEM((NGROUPS, *tile), F32),
-            pltpu.VMEM((2, PAIRS, ROWS, 2 * GROUP), BF16),
-            pltpu.VMEM((2, PAIRS, ROWS, 2 * GROUP), BF16),
+            pltpu.VMEM((2, NGROUPS, ROWS, GROUP), BF16),
+            pltpu.VMEM((2, NGROUPS, ROWS, GROUP), BF16),
             pltpu.VMEM((2, ROWS, BCOLS), F32),
             pltpu.VMEM((2, ROWS, BCOLS), BF16),
             pltpu.VMEM((2, ROWS, BCOLS), BF16),
@@ -488,13 +509,11 @@
             pltpu.VMEM((2, NN - 1, 8, ROWS), F32),
             pltpu.VMEM((2, SAMPLES, ROWS), F32),
             pltpu.VMEM((2, 2 * SAMPLES, ROWS), BF16),
-            pltpu.VMEM((4, 2, 2, *tile), F32),
-            pltpu.VMEM((4, 2, 2, *tile), F32),
-            pltpu.VMEM((4, 2, 2, *tile), F32),
-            pltpu.VMEM((4, 2, 2, *tile), F32),
-            pltpu.VMEM((3, 2, 2, *tile), F32),
-            pltpu.VMEM((2, 2, *tile), F32),
-            pltpu.VMEM((2, *tile), F32),
+            pltpu.VMEM((8, 2, *tile), F32),
+            pltpu.VMEM((8, 2, *tile), F32),
+            pltpu.VMEM((8, 2, *tile), F32),
+            pltpu.VMEM((7, 2, *tile), F32),
+            pltpu.VMEM((NGROUPS, D, GROUP), F32),
             dma,
             dma((4, NW)),
             dma((4, NW)),
@@ -502,15 +521,27 @@
             dma((4, NN)),
             dma((NN,)),
             dma((1,)),
-            dma((5,)),
-            dma((5,)),
+            dma((8,)),
+            dma((8,)),
+            dma((8,)),
+            dma((8,)),
         ],
         compiler_params=pltpu.CompilerParams(collective_id=0, has_side_effects=True),
         name="posterior",
     )(
-        place, mine, scales, ordered, row_points, frequencies, phases.reshape(1, -1), feature_weights,
+        order, place, mine, scales, points, frequencies, phases.reshape(1, -1), feature_weights,
         targets.reshape(1, -1), noise, inverses,
     )
+    return pl.pallas_call(
+        unpack,
+        out_shape=(
+            jax.ShapeDtypeStruct((SAMPLES, 2 * GROUP), F32),
+            jax.ShapeDtypeStruct((2, SAMPLES, ROWS), F32),
+        ),
+        in_specs=[vmem],
+        out_specs=(vmem, vmem),
+        name="unpack",
+    )(result)
 
 
 def solution(mesh):

time: 85.1 us -> 74.5 us (0.88)
  Pallas kernels: 81.1 us -> 73.1 us
  local copies, waits for them, and re-layouts: 3.14 us -> 0 us
    pallas_call x2 -> x3, Pallas kernels: 81.1 us -> 73.1 us  [the longest x1 70 us: on_device(): pl.pallas_call(body, out_shape=jax.ShapeDtypeStruct((SAMPLES, 2 * GROUP +...]
    unnamed x2 -> x0, local copies, waits for them, and re-layouts: 3.14 us -> none
where the time goes in v2:
time: 74.5 us; the launch traced here: 73.8 us
  Pallas kernels  73.1 us (98%)
    pallas_call x1, Pallas kernels, on_device(): pl.pallas_call(body, out_shape=jax.ShapeDtypeStruct((SAMPLES, 2 * GROUP +...  70 us
    pallas_call x1, Pallas kernels, on_device(): pl.pallas_call(unpack, out_shape=(jax.ShapeDtypeStruct((SAMPLES, 2 * GROU...  1.7 us

profile of v2, /device:TPU:1, one launch (start us, length us, event | category | flops | bytes accessed | tf_op | source)
XLA Modules:
  0.0 73.8 jit_solution(13244024290895589165)
XLA Ops:
  0.6 1.4 %arrange.1 = (s32[40]{0:T(128)}, s32[32]{0:T(128)}, f32[64]{0:T(128)}) custom-call(s32[2,64]{1,0:T(2,128)} %groups.1), custom_call_target="tpu_custom_call" | custom-call | tf_op jit(solution)/shard_map/arrange/pallas_call | solution.py:476
  2.1 70.0 %posterior.1.result = f32[64,1280]{1,0:T(8,128)} custom-call(s32[40]{0:T(128)} %get-tuple-element.5.order, s32[32]{0:T(128)} %get-tuple-element.6.place, f32[64]{0:T(128)} %get-tuple-element.7.mine, f32[8]{0:T(128)} %scales.1, f32[8,4096]{1,0:T(8,128)} %points.1, f32[8,2048]{1,0:T(8,128)} %freq.1, f32[1,2048]{1,0:T(1,128)} %bitcast.2, bf16[64,2048]{1,0:T(8,128)(2,1)} %fw.1, ...), custom_call_target="tpu_custom_call" | custom-call | tf_op jit(solution)/shard_map/posterior/pallas_call | solution.py:487
  72.1 1.7 %unpack.1 = (f32[64,256]{1,0:T(8,128)}, f32[2,64,512]{2,1,0:T(8,128)}) custom-call(f32[64,1280]{1,0:T(8,128)} %posterior.1.result), custom_call_target="tpu_custom_call" | custom-call | tf_op jit(solution)/shard_map/unpack/pallas_call | solution.py:535

commit v3 on v2

--- a/solution.py
+++ b/solution.py
@@ -27,6 +27,8 @@
 LN2 = math.log(2.0)
 LOG2E = 1.0 / LN2
 ROUND = 12582912.0
+WIDE_ORDER = (12, 13, 10, 11, 14, 15, 4, 5, 8, 9, 2, 3, 6, 7, 1)
+NARROW_ORDER = (6, 5, 7, 2, 1, 3, 4)
 SIN = (6.283185005, -41.34165573, 81.60100555, -76.54978180, 39.53670502)
 
 
@@ -123,23 +125,28 @@
     coord_scale = scale_col * (math.sqrt(5.0) * LOG2E)
     ones = jnp.ones((1, GROUP), F32)
 
-    @pl.loop(0, FHERE // GROUP)
-    def _(k):
-        at = pl.ds(pl.multiple_of(k * GROUP, GROUP), GROUP)
+    for k in range(FHERE // GROUP):
+        at = slice(k * GROUP, (k + 1) * GROUP)
         f = freq[:, at] * (0.5 / math.pi)
         ph = split3(phases[:, at] * (0.5 / math.pi))
         amat[at, :] = left_stack(f, rows_of(*ph)).T.astype(BF16)
 
-    @pl.loop(0, NGROUPS)
-    def _(g):
-        at = pl.ds(pl.multiple_of(g * GROUP, GROUP), GROUP)
-        here = points[:, at]
-        pts[g] = here
-        bmat[g] = right_stack(here, rows_of(ones, ones, ones)).astype(BF16)
-        z = (here - 0.5) * coord_scale
-        t = split3(jnp.sum(z * z, axis=0, keepdims=True))
-        cmat[g] = right_stack(z, rows_of(ones, ones, ones, *t)).astype(BF16)
-
+    for g in range(NGROUPS):
+        pts[g] = points[:, g * GROUP : (g + 1) * GROUP]
+
+    def point_operands(lo, hi):
+        @pl.loop(lo, hi, unroll=4)
+        def _(k):
+            bmat[k] = right_stack(pts[order[k]], rows_of(ones, ones, ones)).astype(BF16)
+
+    def kernel_operands():
+        @pl.loop(0, NGROUPS, unroll=4)
+        def _(k):
+            z = (pts[order[k]] - 0.5) * coord_scale
+            t = split3(jnp.sum(z * z, axis=0, keepdims=True))
+            cmat[k] = right_stack(z, rows_of(ones, ones, ones, *t)).astype(BF16)
+
+    point_operands(0, 8)
     for i in range(2):
         at = slice(i * GROUP, (i + 1) * GROUP)
         base[i] = targets[:, at] - noise[:, at]
@@ -147,7 +154,7 @@
     def prior_pairs(lo, hi):
         @pl.loop(lo, hi)
         def _(pair):
-            rhs = jnp.concatenate([bmat[order[2 * pair]], bmat[order[2 * pair + 1]]], axis=1)
+            rhs = jnp.concatenate([bmat[2 * pair], bmat[2 * pair + 1]], axis=1)
             acc = jnp.zeros((SAMPLES, 2 * GROUP), F32)
             for k in range(FHERE // FCHUNK):
                 at = slice(k * FCHUNK, (k + 1) * FCHUNK)
@@ -162,7 +169,7 @@
     def kernel_pairs(lo, hi):
         @pl.loop(lo, hi)
         def _(pair):
-            rhs = jnp.concatenate([cmat[order[2 * pair]], cmat[order[2 * pair + 1]]], axis=1)
+            rhs = jnp.concatenate([cmat[2 * pair], cmat[2 * pair + 1]], axis=1)
             for b in range(2):
                 for k in range(2):
                     at = slice(k * 256, (k + 1) * 256)
@@ -180,43 +187,50 @@
     def wide_chunk(ref, peer):
         return ref.at[lax.div(peer, 2), pl.ds(pl.multiple_of(lax.rem(peer, 2) * 32, 32), 32)]
 
-    def wide_copy(b, phase, d, gather):
-        peer = lax.rem(w + d, NW)
-        k = 2 * b + phase
+    def wide_peer(rel, sign):
+        z, x, c = rel // 8, rel // 2 % 4, rel % 2
+        return (
+            lax.rem(z_here + z, 2) * 8 + lax.rem(x_here + (x if sign > 0 else 4 - x), 4) * 2 + lax.rem(core + c, 2)
+        )
+
+    def narrow_peer(rel, sign):
+        z, y = rel // 4, rel % 4
+        return lax.rem(lax.div(n, 4) + z, 2) * 4 + lax.rem(lax.rem(n, 4) + (y if sign > 0 else 4 - y), 4)
+
+    def wide_copy(b, gather, rel):
+        peer = wide_peer(rel, 1)
+        k = 2 * b + gather
         if gather:
             src = wide_chunk(r_buf.at[b], w)
             dst = wide_chunk(r_buf.at[b], w)
         else:
             src = wide_chunk(q.at[pl.ds(8 * b, 8)], peer)
-            dst = rs_buf.at[b, d - 1]
-        return pltpu.make_async_remote_copy(
-            src_ref=src, dst_ref=dst, send_sem=wsend.at[k, d], recv_sem=wrecv.at[k, d],
+            dst = rs_buf.at[b, rel - 1]
+        return pltpu.make_async_remote_copy(
+            src_ref=src, dst_ref=dst, send_sem=wsend.at[k, rel], recv_sem=wrecv.at[k, rel],
             device_id=wide_dev(peer), device_id_type=MESH,
         )
 
-    def wide_arrival(b, phase, d, gather):
-        peer = lax.rem(w + NW - d, NW)
-        k = 2 * b + phase
-        dst = wide_chunk(r_buf.at[b], peer) if gather else rs_buf.at[b, d - 1]
-        return pltpu.make_async_remote_copy(
-            src_ref=dst, dst_ref=dst, send_sem=wsend.at[k, d], recv_sem=wrecv.at[k, d],
+    def wide_arrival(b, gather, rel):
+        peer = wide_peer(rel, -1)
+        k = 2 * b + gather
+        dst = wide_chunk(r_buf.at[b], peer) if gather else rs_buf.at[b, rel - 1]
+        return pltpu.make_async_remote_copy(
+            src_ref=dst, dst_ref=dst, send_sem=wsend.at[k, rel], recv_sem=wrecv.at[k, rel],
             device_id=wide_dev(peer), device_id_type=MESH,
         )
 
     def start_wide(b, gather):
-        @pl.loop(1, NW)
-        def _(d):
-            wide_copy(b, int(gather), d, gather).start()
+        for rel in WIDE_ORDER:
+            wide_copy(b, gather, rel).start()
 
     def end_wide(b, gather):
-        @pl.loop(1, NW)
-        def _(d):
-            wide_arrival(b, int(gather), d, gather).wait_recv()
+        for rel in reversed(WIDE_ORDER):
+            wide_arrival(b, gather, rel).wait_recv()
 
     def end_sends(b):
-        @pl.loop(1, NW)
-        def _(d):
-            wide_copy(b, 0, d, False).wait_send()
+        for rel in WIDE_ORDER:
+            wide_copy(b, 0, rel).wait_send()
 
     def sum_wide(b):
         total = wide_chunk(q.at[pl.ds(8 * b, 8)], w)[...]
@@ -224,39 +238,37 @@
             total = total + rs_buf[b, d]
         wide_chunk(r_buf.at[b], w)[...] = total
 
-    def narrow_copy(b, phase, d):
-        peer = lax.rem(n + d, NN)
+    def narrow_copy(b, phase, rel):
+        peer = narrow_peer(rel, 1)
         k = 2 * b + phase
         mine = pl.ds(pl.multiple_of(n * 8, 8), 8)
         theirs = pl.ds(pl.multiple_of(peer * 8, 8), 8)
         if phase:
             src, dst = wf.at[b, mine], wf.at[b, mine]
         else:
-            src, dst = wp.at[b, theirs], nb.at[b, d - 1]
-        return pltpu.make_async_remote_copy(
-            src_ref=src, dst_ref=dst, send_sem=nsend.at[k, d], recv_sem=nrecv.at[k, d],
+            src, dst = wp.at[b, theirs], nb.at[b, rel - 1]
+        return pltpu.make_async_remote_copy(
+            src_ref=src, dst_ref=dst, send_sem=nsend.at[k, rel], recv_sem=nrecv.at[k, rel],
             device_id=narrow_dev(peer), device_id_type=MESH,
         )
 
-    def narrow_arrival(b, phase, d):
-        peer = lax.rem(n + NN - d, NN)
+    def narrow_arrival(b, phase, rel):
+        peer = narrow_peer(rel, -1)
         k = 2 * b + phase
         theirs = pl.ds(pl.multiple_of(peer * 8, 8), 8)
-        dst = wf.at[b, theirs] if phase else nb.at[b, d - 1]
-        return pltpu.make_async_remote_copy(
-            src_ref=dst, dst_ref=dst, send_sem=nsend.at[k, d], recv_sem=nrecv.at[k, d],
+        dst = wf.at[b, theirs] if phase else nb.at[b, rel - 1]
+        return pltpu.make_async_remote_copy(
+            src_ref=dst, dst_ref=dst, send_sem=nsend.at[k, rel], recv_sem=nrecv.at[k, rel],
             device_id=narrow_dev(peer), device_id_type=MESH,
         )
 
     def start_narrow(b, phase):
-        @pl.loop(1, NN)
-        def _(d):
-            narrow_copy(b, phase, d).start()
+        for rel in NARROW_ORDER:
+            narrow_copy(b, phase, rel).start()
 
     def end_narrow(b, phase):
-        @pl.loop(1, NN)
-        def _(d):
-            narrow_arrival(b, phase, d).wait_recv()
+        for rel in reversed(NARROW_ORDER):
+            narrow_arrival(b, phase, rel).wait_recv()
 
     def sum_narrow(b):
         mine = pl.ds(pl.multiple_of(n * 8, 8), 8)
@@ -313,7 +325,7 @@
 
     prior_pairs(0, 4)
     pl.semaphore_wait(barrier, NW - 1 + NN - 1)
-    start_wide(0, False)
+    start_wide(0, 0)
     holder = n == lax.div(w, 2)
 
     @pl.when(holder)
@@ -325,10 +337,11 @@
         def _(d):
             rows_copy(d).start()
 
+    point_operands(8, 16)
     prior_pairs(4, 8)
-    end_wide(0, False)
+    end_wide(0, 0)
     sum_wide(0)
-    start_wide(0, True)
+    start_wide(0, 1)
 
     @pl.when(jnp.logical_not(holder))
     def _():
@@ -337,6 +350,8 @@
             device_id=narrow_dev(lax.rem(n + 1, NN)), device_id_type=MESH,
         ).wait_recv()
 
+    point_operands(16, NGROUPS)
+    kernel_operands()
     for k in range(8):
         z = (rows[k] - 0.5) * coord_scale
         t = split3(jnp.sum(z * z, axis=0, keepdims=True))
@@ -354,40 +369,42 @@
         inv_hi[b, at, :] = hi_part
         inv_lo[b, at, :] = (value - hi_part.astype(F32)).astype(BF16)
 
-    kernel_pairs(4, 8)
-    prior_pairs(8, 10)
-    end_wide(0, True)
+    kernel_pairs(4, 6)
+    end_wide(0, 1)
     solve(0)
     start_narrow(0, 0)
-    prior_pairs(10, 12)
+    kernel_pairs(6, 8)
+    prior_pairs(8, 10)
     end_narrow(0, 0)
     sum_narrow(0)
     start_narrow(0, 1)
-    prior_pairs(12, 14)
+    prior_pairs(10, 13)
     end_narrow(0, 1)
     finish_weights(0)
     apply_pairs(0, 4, 8)
-    start_wide(1, False)
-    prior_pairs(14, 16)
-    kernel_pairs(0, 4)
-    end_wide(1, False)
+    start_wide(1, 0)
+    prior_pairs(13, 16)
+    kernel_pairs(0, 2)
+    end_wide(1, 0)
     sum_wide(1)
-    start_wide(1, True)
-    kernel_pairs(8, 16)
-    end_wide(1, True)
+    start_wide(1, 1)
+    kernel_pairs(2, 4)
+    kernel_pairs(8, 13)
+    end_wide(1, 1)
     solve(1)
     start_narrow(1, 0)
+    kernel_pairs(13, 16)
     end_sends(0)
     apply_pairs(0, 0, 4)
     apply_noise(0)
-    apply_pairs(0, 8, 16)
     end_narrow(1, 0)
     sum_narrow(1)
     start_narrow(1, 1)
+    apply_pairs(0, 8, 16)
+    end_sends(1)
     end_narrow(1, 1)
     finish_weights(1)
 
-    end_sends(1)
     apply_noise(1)
 
     def chip(rel):
@@ -410,16 +427,17 @@
             device_id=wide_dev(chip(rel) + core), device_id_type=MESH,
         )
 
-    @pl.loop(0, 8)
-    def _(j):
-        rel = 7 - j
+    def for_other(rel):
         piece = final_piece(chip(rel) + 1 - core)
         for i in range(2):
             give[rel, i] = piece[i]
         core_copy(rel).start()
 
+    for_other(7)
+
     @pl.loop(0, 7)
     def _(j):
+        for_other(6 - j)
         rel = 7 - j
         piece = final_piece(chip(rel) + core)
         core_copy(rel).wait_recv()
@@ -436,16 +454,12 @@
     for i in range(2):
         result[:, i * GROUP : (i + 1) * GROUP] = total[i]
 
-    @pl.loop(1, NW)
-    def _(d):
-        wide_copy(0, 1, d, True).wait_send()
-        wide_copy(1, 1, d, True).wait_send()
-
-    @pl.loop(1, NN)
-    def _(d):
-        for b in range(2):
+    for b in range(2):
+        for rel in WIDE_ORDER:
+            wide_copy(b, 1, rel).wait_send()
+        for rel in NARROW_ORDER:
             for phase in range(2):
-                narrow_copy(b, phase, d).wait_send()
+                narrow_copy(b, phase, rel).wait_send()
 
     @pl.when(holder)
     def _():

time: 74.5 us -> 70.7 us (0.949)
  Pallas kernels: 73.1 us -> 69.9 us
    pallas_call x1, Pallas kernels: 70 us -> 66.7 us  [on_device(): pl.pallas_call(body, out_shape=jax.ShapeDtypeStruct((SAMPLES, 2 * GROUP +...]
where the time goes in v3:
time: 70.7 us; the launch traced here: 70.5 us
  Pallas kernels  69.9 us (99%)
    pallas_call x1, Pallas kernels, on_device(): pl.pallas_call(body, out_shape=jax.ShapeDtypeStruct((SAMPLES, 2 * GROUP +...  66.7 us
    pallas_call x1, Pallas kernels, on_device(): pl.pallas_call(unpack, out_shape=(jax.ShapeDtypeStruct((SAMPLES, 2 * GROU...  1.7 us
    pallas_call x1, Pallas kernels, on_device(): pl.pallas_call(arrange, out_shape=(jax.ShapeDtypeStruct((NGROUPS + 8,), j...  1.45 us

profile of v3, /device:TPU:1, one launch (start us, length us, event | category | flops | bytes accessed | tf_op | source)
XLA Modules:
  0.0 70.5 jit_solution(11358752606536575245)
XLA Ops:
  0.6 1.4 %arrange.1 = (s32[40]{0:T(128)}, s32[32]{0:T(128)}, f32[64]{0:T(128)}) custom-call(s32[2,64]{1,0:T(2,128)} %groups.1), custom_call_target="tpu_custom_call" | custom-call | tf_op jit(solution)/shard_map/arrange/pallas_call | solution.py:490
  2.1 66.7 %posterior.1.result = f32[64,1280]{1,0:T(8,128)} custom-call(s32[40]{0:T(128)} %get-tuple-element.5.order, s32[32]{0:T(128)} %get-tuple-element.6.place, f32[64]{0:T(128)} %get-tuple-element.7.mine, f32[8]{0:T(128)} %scales.1, f32[8,4096]{1,0:T(8,128)} %points.1, f32[8,2048]{1,0:T(8,128)} %freq.1, f32[1,2048]{1,0:T(1,128)} %bitcast.2, bf16[64,2048]{1,0:T(8,128)(2,1)} %fw.1, ...), custom_call_target="tpu_custom_call" | custom-call | tf_op jit(solution)/shard_map/posterior/pallas_call | solution.py:501
  68.8 1.7 %unpack.1 = (f32[64,256]{1,0:T(8,128)}, f32[2,64,512]{2,1,0:T(8,128)}) custom-call(f32[64,1280]{1,0:T(8,128)} %posterior.1.result), custom_call_target="tpu_custom_call" | custom-call | tf_op jit(solution)/shard_map/unpack/pallas_call | solution.py:549
